TPU v7x, 32 devices: a whole 2x2x4 slice. The times are simulated.
32 devices in a mesh: row: 8 (over z, y), col: 4 (over x, core).
Axes of the slice: x: 2, y: 2, z: 4, core: 2. Of those that a mesh axis runs over, the one named last changes fastest.
Arguments:
- sequence: bfloat16 [128, 1024], P('row'), may hold values from -6 to 6
- pair_state: bfloat16 [128, 128, 128], P('row', 'col'), may hold values from -6 to 6
- residue_mask: int32 [128], replicated, may hold values 0 or 1
- chain_index: int32 [128], replicated, may hold values from 0 to 3, never falling along the last dimension, each value on 1 to 64 neighbouring positions
- attention_in: bfloat16 [1024, 4, 1024], P(None, None, 'col'), may hold values from -0.1875 to 0.1875
- attention_out: bfloat16 [1024, 1024], P('col'), may hold values from -0.1875 to 0.1875
- bias_weight: bfloat16 [128, 32], replicated, may hold values from -40 to 40
- chain_bias: float32 [32], replicated, may hold values from -2 to 2
- outer_in: bfloat16 [1024, 128], replicated, may hold values from -0.1875 to 0.1875
- outer_out: bfloat16 [128, 128], replicated, may hold values from -0.5 to 0.5
- triangle_in: bfloat16 [128, 5, 128], replicated, may hold values from -0.5 to 0.5
- triangle_out: bfloat16 [128, 128], replicated, may hold values from -0.5 to 0.5
- transition_up: bfloat16 [128, 512], replicated, may hold values from -0.5 to 0.5
- transition_down: bfloat16 [512, 128], replicated, may hold values from -0.25 to 0.25
Outputs:
- sequence_out: bfloat16 [128, 1024], P('row')
- pair_out: bfloat16 [128, 128, 128], P('row', 'col')
Inputs may be any that keep to these rules, and one draw needn't show every extreme that they name: chain_index never falls along the residues; each chain holds at most 64 residues.
All inputs are finite; a program needn't handle non-finite values.
Results may differ from a plain program's by a relative error of at most 0.0095.
The roundings to bfloat16 on the way count: a program that leaves them out, or rounds other values in their place, can miss the bound.
Values may be sent and summed in bfloat16 or wider, within the bound.
A program may use at most 64 MiB of HBM per device.

v0:
```python
import math
import jax
import jax.numpy as jnp
from jax import lax
from jax.sharding import PartitionSpec as P


def layer_norm(values):
    center = values - jnp.mean(values, axis=-1, keepdims=True)
    spread = jnp.mean(center * center, axis=-1, keepdims=True)
    return center * lax.rsqrt(spread + 1e-05)


def per_device(
    sequence,
    pair_state,
    residue_mask,
    chain_index,
    attention_in,
    attention_out,
    bias_weight,
    chain_bias,
    outer_in,
    outer_out,
    triangle_in,
    triangle_out,
    transition_up,
    transition_down,
):
    rows_here, cols_here, channels = pair_state.shape
    length_all = residue_mask.shape[0]
    row_index = lax.axis_index("row")
    col_index = lax.axis_index("col")
    row_start = row_index * rows_here
    col_start = col_index * cols_here
    pair_wide = pair_state.astype(jnp.float32)
    normed_pair = layer_norm(pair_wide).astype(jnp.bfloat16)
    bias_tile = jnp.einsum(
        "ijc,ch->hij", normed_pair, bias_weight, preferred_element_type=jnp.float32
    )
    pair_bias = lax.all_to_all(bias_tile, "col", split_axis=0, concat_axis=2, tiled=True)
    heads_here = pair_bias.shape[0]
    normed_seq = layer_norm(sequence.astype(jnp.float32)).astype(jnp.bfloat16)
    projected = jnp.einsum(
        "id,dpe->ipe", normed_seq, attention_in, preferred_element_type=jnp.float32
    )
    query = projected[:, 0].astype(jnp.bfloat16)
    key_rows = projected[:, 1].astype(jnp.bfloat16)
    value_rows = projected[:, 2].astype(jnp.bfloat16)
    gate = jax.nn.sigmoid(projected[:, 3])
    keys_all, values_all = (
        lax.all_gather(key_rows, "row", axis=0, tiled=True),
        lax.all_gather(value_rows, "row", axis=0, tiled=True),
    )
    head_width = query.shape[1] // heads_here
    query_heads = query.reshape(rows_here, heads_here, head_width)
    key_heads = keys_all.reshape(length_all, heads_here, head_width)
    value_heads = values_all.reshape(length_all, heads_here, head_width)
    scale = 1.0 / math.sqrt(head_width)
    scores = (
        jnp.einsum("ihd,jhd->hij", query_heads, key_heads, preferred_element_type=jnp.float32)
        * scale
    )
    chain_rows = lax.dynamic_slice_in_dim(chain_index, row_start, rows_here, 0)
    same_chain = (chain_rows[:, None] == chain_index[None, :]).astype(jnp.float32)
    head_offset = lax.dynamic_slice_in_dim(chain_bias, col_index * heads_here, heads_here, 0)
    scores = scores + pair_bias + head_offset[:, None, None] * same_chain[None]
    positions = jnp.arange(length_all, dtype=jnp.int32)
    query_ids = row_start + jnp.arange(rows_here, dtype=jnp.int32)
    allowed = (residue_mask[None, :] == 1) | (query_ids[:, None] == positions[None, :])
    allowed = allowed[None]
    highest = jnp.max(jnp.where(allowed, scores, -jnp.inf), axis=-1, keepdims=True)
    raised = jnp.where(allowed, jnp.exp(scores - highest), 0.0)
    weights = (raised / jnp.sum(raised, axis=-1, keepdims=True)).astype(jnp.bfloat16)
    gathered = jnp.einsum(
        "hij,jhd->ihd", weights, value_heads, preferred_element_type=jnp.float32
    ).reshape(rows_here, -1)
    mixed = (gate * gathered).astype(jnp.bfloat16)
    head_terms = jnp.dot(mixed, attention_out, preferred_element_type=jnp.float32)
    update = lax.psum(head_terms, "col")
    sequence_out = (sequence.astype(jnp.float32) + update).astype(jnp.bfloat16)
    normed_out = layer_norm(sequence_out.astype(jnp.float32)).astype(jnp.bfloat16)
    outer_rows = jnp.dot(normed_out, outer_in, preferred_element_type=jnp.float32).astype(
        jnp.bfloat16
    )
    half_width = outer_rows.shape[1] // 2
    right_all = lax.all_gather(outer_rows[:, half_width:], "row", axis=0, tiled=True)
    right_side = lax.dynamic_slice_in_dim(right_all, col_start, cols_here, 0).astype(jnp.float32)
    left_side = outer_rows[:, :half_width].astype(jnp.float32)
    outer_feat = jnp.concatenate(
        [
            left_side[:, None, :] * right_side[None, :, :],
            left_side[:, None, :] - right_side[None, :, :],
        ],
        axis=-1,
    ).astype(jnp.bfloat16)
    pair_mid = pair_wide + jnp.dot(
        outer_feat.reshape(-1, 2 * half_width), outer_out, preferred_element_type=jnp.float32
    ).reshape(rows_here, cols_here, channels)
    normed_mid = layer_norm(pair_mid).astype(jnp.bfloat16)
    tri = jnp.dot(
        normed_mid.reshape(-1, channels),
        triangle_in.reshape(channels, -1),
        preferred_element_type=jnp.float32,
    ).reshape(rows_here, cols_here, 5, channels)
    live = residue_mask.astype(jnp.float32)
    row_live = lax.dynamic_slice_in_dim(live, row_start, rows_here, 0)
    col_live = lax.dynamic_slice_in_dim(live, col_start, cols_here, 0)
    pair_live = (row_live[:, None] * col_live[None, :])[:, :, None]
    left_op = (jax.nn.sigmoid(tri[:, :, 0]) * tri[:, :, 1] * pair_live).astype(jnp.bfloat16)
    right_op = (jax.nn.sigmoid(tri[:, :, 2]) * tri[:, :, 3] * pair_live).astype(jnp.bfloat16)
    out_gate = jax.nn.sigmoid(tri[:, :, 4])
    column_all = lax.all_gather(right_op, "row", axis=0, tiled=True)
    crossed = lax.psum_scatter(
        jnp.einsum("jkc,ikc->jic", column_all, left_op, preferred_element_type=jnp.float32),
        "col",
        scatter_dimension=0,
        tiled=True,
    )
    product = jnp.transpose(crossed, (1, 0, 2))
    normed_product = layer_norm(product).astype(jnp.bfloat16)
    projected_product = jnp.dot(
        normed_product.reshape(-1, channels), triangle_out, preferred_element_type=jnp.float32
    ).reshape(rows_here, cols_here, channels)
    pair_late = pair_mid + out_gate * projected_product
    normed_late = layer_norm(pair_late).astype(jnp.bfloat16)
    hidden = jax.nn.relu(
        jnp.dot(
            normed_late.reshape(-1, channels), transition_up, preferred_element_type=jnp.float32
        )
    ).astype(jnp.bfloat16)
    lowered = jnp.dot(hidden, transition_down, preferred_element_type=jnp.float32).reshape(
        rows_here, cols_here, channels
    )
    pair_out = (pair_late + lowered).astype(jnp.bfloat16)
    return (sequence_out, pair_out)


def solution(mesh):
    return jax.shard_map(
        per_device,
        mesh=mesh,
        in_specs=(
            P("row", None),
            P("row", "col", None),
            P(),
            P(),
            P(None, None, "col"),
            P("col", None),
            P(),
            P(),
            P(),
            P(),
            P(),
            P(),
            P(),
            P(),
        ),
        out_specs=(P("row", None), P("row", "col", None)),
        check_vma=False,
    )
```

profile of v0, /device:TPU:0, one launch (start us, length us, event | category | flops | bytes accessed | tf_op | source)
XLA Modules:
  0.0 257.6 jit_solution(43655018280628967)
XLA Ops:
  7.2 1.2 convert_reduce_fusion
  8.4 1.2 fusion.14
  9.6 1.2 convolution_bitcast_fusion.1
  11.0 0.8 reshape.259
  11.8 4.2 %all-to-all-start = ((f32[4,1,4096]{2,1,0:T(1,128)}), f32[4,1,4096]{2,1,0:T(1,128)S(1)}, u32[]{:S(2)}, u32[]{:S(2)}) async-start(f32[4,1,4096]{2,1,0:T(1,128)} %reshape.259), calls=%async_computation | async-start | bytes 131072 | tf_op jit(solution)/shard_map/all_to_all | solution.py:41
  19.3 0.9 convert_reduce_fusion.1
  20.2 0.9 fusion.50
  21.9 1.9 fusion.92
  24.5 31.5 %all-gather.1 = bf16[128,1,256]{2,0,1:T(8,128)(2,1)S(1)} all-gather(bf16[16,1,256]{2,0,1:T(8,128)(2,1)S(1)} %get-tuple-element.7), channel_id=3, replica_groups=mesh['row'=8,'col'=4] {'row'}, dimensions={0}, use_global_device_ids=true | all-gather | bytes 73728 | tf_op jit(solution)/shard_map/all_gather | solution.py:52
  56.1 30.5 %all-gather = bf16[128,1,256]{2,0,1:T(8,128)(2,1)S(1)} all-gather(bf16[16,1,256]{2,0,1:T(8,128)(2,1)S(1)} %get-tuple-element.8), channel_id=2, replica_groups=mesh['row'=8,'col'=4] {'row'}, dimensions={0}, use_global_device_ids=true | all-gather | bytes 73728 | tf_op jit(solution)/shard_map/all_gather | solution.py:53
  89.2 0.9 fusion.10
  90.4 1.1 convolution_bitcast_fusion.2
  91.6 1.5 fusion.74
  94.0 0.8 copy.95
  94.8 31.4 %all-reduce.2.cloned.1.call-done = f32[16,1024]{1,0:T(8,128)} async-done(((f32[16,1024]{1,0:T(8,128)}), f32[16,1024]{1,0:T(8,128)}) %all-reduce.2.cloned.1.call-update) | async-done | bytes 65552 | tf_op jit(solution)/shard_map/psum | solution.py:80
  126.2 1.0 convert_reduce_fusion.2
  127.7 30.7 %all_gather.14 = bf16[128,64]{1,0:T(8,128)(2,1)S(1)} all-gather(bf16[16,64]{1,0:T(8,128)(2,1)S(1)} %get-tuple-element.12), channel_id=1, replica_groups=mesh['row'=8,'col'=4] {'row'}, dimensions={0}, use_global_device_ids=true | all-gather | bytes 18432 | tf_op jit(solution)/shard_map/all_gather | solution.py:87
  158.4 1.1 fusion.94
  160.3 1.3 fusion.32
  161.6 0.8 fusion.18
  162.5 1.2 copy.101
  163.7 39.1 %all-gather.4.cloned.1.call-done = bf16[128,32,128]{2,1,0:T(8,128)(2,1)} async-done(((bf16[16,32,128]{2,1,0:T(8,128)(2,1)}), bf16[128,32,128]{2,1,0:T(8,128)(2,1)}) %all-gather.4.cloned.1.call-update) | async-done | bytes 1048592 | tf_op jit(solution)/shard_map/all_gather | solution.py:113
  202.8 7.3 %copy.102 = bf16[128,32,128]{1,0,2:T(8,128)(2,1)} copy(bf16[128,32,128]{2,1,0:T(8,128)(2,1)} %all-gather.4.cloned.1.call-done) | data formatting | bytes 2097152 | tf_op jit(solution)/shard_map/all_gather | solution.py:113
  210.0 5.6 %convolution_bitcast_fusion = f32[128,16,128]{0,1,2:T(8,128)} fusion(bf16[16,32,128]{1,0,2:T(8,128)(2,1)} %copy.101, bf16[128,32,128]{1,0,2:T(8,128)(2,1)} %copy.102), kind=kOutput, calls=%fused_computation.4 | convolution fusion | flops 16777216 | bytes 2228224 | tf_op jit(solution)/shard_map/jkc,ikc->jic/dot_general | solution.py:115
  215.6 2.8 %copy.103 = f32[128,16,128]{2,1,0:T(8,128)} copy(f32[128,16,128]{0,1,2:T(8,128)} %convolution_bitcast_fusion) | data formatting | bytes 2097152 | tf_op jit(solution)/shard_map/jkc,ikc->jic/transpose | solution.py:115
  218.4 23.7 %reduce-scatter.2.cloned.1.call-done = f32[32,16,128]{2,1,0:T(8,128)} async-done(((f32[128,16,128]{2,1,0:T(8,128)}), f32[32,16,128]{2,1,0:T(8,128)}) %reduce-scatter.2.cloned.1.call-update) | async-done | bytes 262160 | tf_op jit(solution)/shard_map/reduce_scatter | solution.py:114
  242.1 1.1 bitcast_reduce_fusion
  243.4 1.2 multiply_reduce_fusion.1
  244.7 1.2 multiply_convert_fusion.1
  245.9 1.3 fusion.95
  248.1 1.3 fusion.4
  249.4 1.6 add_convert_fusion
  (76 shorter events, 11.3 us)
Async XLA Ops:
  7.2 14.7 %copy-start = (bf16[1024,4,256]{2,1,0:T(4,128)(2,1)S(1)}, bf16[1024,4,256]{2,1,0:T(4,128)(2,1)}, u32[]{:S(2)}) copy-start(bf16[1024,4,256]{2,1,0:T(4,128)(2,1)} %param.18) | copy-start | bytes 6291460
  9.6 77.8 %copy-start.10 = (f32[32]{0:T(128)S(1)}, f32[32]{0:T(128)}, u32[]{:S(2)}) copy-start(f32[32]{0:T(128)} %param.21) | copy-start | bytes 388
  11.8 75.7 %all-to-all-start = ((f32[4,1,4096]{2,1,0:T(1,128)}), f32[4,1,4096]{2,1,0:T(1,128)S(1)}, u32[]{:S(2)}, u32[]{:S(2)}) async-start(f32[4,1,4096]{2,1,0:T(1,128)} %reshape.259), calls=%async_computation | async-start | bytes 131072 | tf_op jit(solution)/shard_map/all_to_all | solution.py:41
  16.0 110.2 %all-reduce.2.cloned.1.call-start = ((), (), s32[]{:S(2)}) async-start(), calls=%async_computation.2 | async-start | bytes 131072 | tf_op jit(solution)/shard_map/psum | solution.py:80
  21.9 69.8 %copy-start.5 = (bf16[256,1024]{1,0:T(8,128)(2,1)S(1)}, bf16[256,1024]{1,0:T(8,128)(2,1)}, u32[]{:S(2)}) copy-start(bf16[256,1024]{1,0:T(8,128)(2,1)} %param.19) | copy-start | bytes 1572868
  23.7 70.3 %copy-start.6 = (bf16[128,5,128]{2,0,1:T(8,128)(2,1)S(1)}, bf16[128,5,128]{2,0,1:T(8,128)(2,1)}, u32[]{:S(2)}) copy-start(bf16[128,5,128]{2,0,1:T(8,128)(2,1)} %param.24) | copy-start | bytes 491524
  23.7 102.5 %copy-start.4 = (bf16[16,1024]{1,0:T(8,128)(2,1)S(1)}, bf16[16,1024]{1,0:T(8,128)(2,1)}, u32[]{:S(2)}) copy-start(bf16[16,1024]{1,0:T(8,128)(2,1)} %param.14) | copy-start | bytes 98308
  87.4 71.1 %copy-start.3 = (bf16[16,32,128]{2,1,0:T(8,128)(2,1)S(1)}, bf16[16,32,128]{2,1,0:T(8,128)(2,1)}, u32[]{:S(2)}) copy-start(bf16[16,32,128]{2,1,0:T(8,128)(2,1)} %param.15) | copy-start | bytes 393220
  89.2 38.2 %copy-start.8 = (bf16[1024,128]{1,0:T(8,128)(2,1)S(1)}, bf16[1024,128]{1,0:T(8,128)(2,1)}, u32[]{:S(2)}) copy-start(bf16[1024,128]{1,0:T(8,128)(2,1)} %param.22) | copy-start | bytes 786436
  93.2 109.6 %all-gather.4.cloned.1.call-start = ((), (), s32[]{:S(2)}) async-start(), calls=%async_computation.3 | async-start | bytes 1179648 | tf_op jit(solution)/shard_map/all_gather | solution.py:113
  127.2 32.6 %copy-start.7 = (bf16[16,1024]{1,0:T(8,128)(2,1)}, bf16[16,1024]{1,0:T(8,128)(2,1)S(1)}, u32[]{:S(2)}) copy-start(bf16[16,1024]{1,0:T(8,128)(2,1)S(1)} %get-tuple-element.3) | copy-start | bytes 98308
  159.5 0.7 copy-start.2
  162.4 79.7 %reduce-scatter.2.cloned.1.call-start = ((), (), s32[]{:S(2)}) async-start(), calls=%async_computation.4 | async-start | bytes 1310720 | tf_op jit(solution)/shard_map/reduce_scatter | solution.py:114
  245.9 2.2 copy-start.9
  247.2 0.7 copy-start.1
Sparse Core Ops, SparseCore 0:
  93.3 32.8 all-reduce.1
  162.5 40.1 all-gather.3
  218.6 23.5 reduce-scatter.1
where the time goes:
time: 259 us; the launch traced here: 258 us
  waiting for transfers between devices  94.3 us (36%)
  blocking collectives  92.7 us (36%)
  local copies, waits for them, and re-layouts  18.8 us (7%)
  matrix products  17.5 us (7%)
  other arithmetic  16 us (6%)
  between operations  14 us (5%)
  starting transfers between devices  4.32 us (2%)
    all_gather x1, waiting for transfers between devices, per_device(): column_all = lax.all_gather(right_op, 'row', axis=0, tiled=True)  39.1 us
    all_gather x1, blocking collectives, per_device(): lax.all_gather(key_rows, 'row', axis=0, tiled=True)  31.5 us
    psum x1, waiting for transfers between devices, per_device(): update = lax.psum(head_terms, 'col')  31.4 us
    all_gather x1, blocking collectives, per_device(): lax.all_gather(outer_rows[:, half_width:], 'row', axis=0, tiled=True)  30.7 us
    all_gather x1, blocking collectives, per_device(): lax.all_gather(value_rows, 'row', axis=0, tiled=True)  30.5 us
    reduce_scatter x1, waiting for transfers between devices, per_device(): lax.psum_scatter(jnp.einsum('jkc,ikc->jic', column_all, left_op, preferre...  23.7 us
    all_gather x1, local copies, waits for them, and re-layouts, per_device(): column_all = lax.all_gather(right_op, 'row', axis=0, tiled=True)  7.25 us
    dot_general x1, matrix products, per_device(): jnp.einsum('jkc,ikc->jic', column_all, left_op, preferred_element_type=jn...  5.6 us
  transfers between devices with their start and end apart: 4, of which 3 were waited for; matrix products, arithmetic and copies ran while one was open for 5% of the time, Pallas kernels for 0%

commit v1 on v0

--- a/solution.py
+++ b/solution.py
@@ -77,7 +77,9 @@
     ).reshape(rows_here, -1)
     mixed = (gate * gathered).astype(jnp.bfloat16)
     head_terms = jnp.dot(mixed, attention_out, preferred_element_type=jnp.float32)
-    update = lax.psum(head_terms, "col")
+    update = head_terms
+    for hop in (1, 2):
+        update = update + lax.ppermute(update, "col", [(dev, dev ^ hop) for dev in range(4)])
     sequence_out = (sequence.astype(jnp.float32) + update).astype(jnp.bfloat16)
     normed_out = layer_norm(sequence_out.astype(jnp.float32)).astype(jnp.bfloat16)
     outer_rows = jnp.dot(normed_out, outer_in, preferred_element_type=jnp.float32).astype(

time: 259 us -> 229 us (0.88)
  waiting for transfers between devices: 94.3 us -> 66.1 us
    psum x1 -> x0, waiting for transfers between devices: 31.4 us -> none  [per_device(): update = lax.psum(head_terms, 'col')]
  transfers between devices with their start and end apart: 4 -> 5, of which waited for: 3 -> 4; matrix products, arithmetic and copies ran while one was open for 5% -> 5% of each run, Pallas kernels for 0% -> 0%
where the time goes in v1:
time: 229 us; the launch traced here: 228 us
  blocking collectives  92.6 us (40%)
  waiting for transfers between devices  66.1 us (29%)
  local copies, waits for them, and re-layouts  17.7 us (8%)
  matrix products  16.9 us (7%)
  other arithmetic  14.5 us (6%)
  between operations  14.3 us (6%)
  starting transfers between devices  6.27 us (3%)
    all_gather x1, waiting for transfers between devices, per_device(): column_all = lax.all_gather(right_op, 'row', axis=0, tiled=True)  40.4 us
    all_gather x1, blocking collectives, per_device(): lax.all_gather(key_rows, 'row', axis=0, tiled=True)  31.5 us
    all_gather x1, blocking collectives, per_device(): lax.all_gather(outer_rows[:, half_width:], 'row', axis=0, tiled=True)  30.6 us
    all_gather x1, blocking collectives, per_device(): lax.all_gather(value_rows, 'row', axis=0, tiled=True)  30.5 us
    reduce_scatter x1, waiting for transfers between devices, per_device(): lax.psum_scatter(jnp.einsum('jkc,ikc->jic', column_all, left_op, preferre...  23.7 us
    all_gather x1, local copies, waits for them, and re-layouts, per_device(): column_all = lax.all_gather(right_op, 'row', axis=0, tiled=True)  7.25 us
    dot_general x1, matrix products, per_device(): jnp.einsum('jkc,ikc->jic', column_all, left_op, preferred_element_type=jn...  5.6 us
  transfers between devices with their start and end apart: 5, of which 4 were waited for; matrix products, arithmetic and copies ran while one was open for 5% of the time, Pallas kernels for 0%

profile of v1, /device:TPU:0, one launch (start us, length us, event | category | flops | bytes accessed | tf_op | source)
XLA Modules:
  0.0 228.5 jit_solution(8431120564355698262)
XLA Ops:
  7.2 1.2 convert_reduce_fusion
  8.4 1.2 fusion.14
  9.6 1.2 convolution_bitcast_fusion.1
  11.0 0.8 reshape.259
  11.8 4.2 %all-to-all-start = ((f32[4,1,4096]{2,1,0:T(1,128)}), f32[4,1,4096]{2,1,0:T(1,128)S(1)}, u32[]{:S(2)}, u32[]{:S(2)}) async-start(f32[4,1,4096]{2,1,0:T(1,128)} %reshape.259), calls=%async_computation | async-start | bytes 131072 | tf_op jit(solution)/shard_map/all_to_all | solution.py:41
  16.7 0.9 convert_reduce_fusion.1
  17.6 0.9 fusion.50
  20.0 1.9 fusion.92
  22.6 31.5 %all-gather.1 = bf16[128,1,256]{2,0,1:T(8,128)(2,1)S(1)} all-gather(bf16[16,1,256]{2,0,1:T(8,128)(2,1)S(1)} %get-tuple-element.7), channel_id=3, replica_groups=mesh['row'=8,'col'=4] {'row'}, dimensions={0}, use_global_device_ids=true | all-gather | bytes 73728 | tf_op jit(solution)/shard_map/all_gather | solution.py:52
  54.2 30.5 %all-gather = bf16[128,1,256]{2,0,1:T(8,128)(2,1)S(1)} all-gather(bf16[16,1,256]{2,0,1:T(8,128)(2,1)S(1)} %get-tuple-element.8), channel_id=2, replica_groups=mesh['row'=8,'col'=4] {'row'}, dimensions={0}, use_global_device_ids=true | all-gather | bytes 73728 | tf_op jit(solution)/shard_map/all_gather | solution.py:53
  87.4 0.9 fusion.10
  88.5 1.1 convolution_bitcast_fusion.2
  89.8 0.9 fusion.74
  92.0 2.0 collective-permute-start.1
  94.0 0.8 copy.95
  94.8 1.5 collective-permute-done.1
  97.0 30.6 %all_gather.14 = bf16[128,64]{1,0:T(8,128)(2,1)S(1)} all-gather(bf16[16,64]{1,0:T(8,128)(2,1)S(1)} %get-tuple-element.12), channel_id=1, replica_groups=mesh['row'=8,'col'=4] {'row'}, dimensions={0}, use_global_device_ids=true | all-gather | bytes 18432 | tf_op jit(solution)/shard_map/all_gather | solution.py:89
  127.7 1.1 fusion.94
  129.5 1.3 fusion.32
  130.8 0.8 fusion.18
  131.7 1.2 copy.101
  132.9 40.4 %all-gather.4.cloned.1.call-done = bf16[128,32,128]{2,1,0:T(8,128)(2,1)} async-done(((bf16[16,32,128]{2,1,0:T(8,128)(2,1)}), bf16[128,32,128]{2,1,0:T(8,128)(2,1)}) %all-gather.4.cloned.1.call-update) | async-done | bytes 1048592 | tf_op jit(solution)/shard_map/all_gather | solution.py:115
  173.3 7.3 %copy.102 = bf16[128,32,128]{1,0,2:T(8,128)(2,1)} copy(bf16[128,32,128]{2,1,0:T(8,128)(2,1)} %all-gather.4.cloned.1.call-done) | data formatting | bytes 2097152 | tf_op jit(solution)/shard_map/all_gather | solution.py:115
  180.6 5.6 %convolution_bitcast_fusion = f32[128,16,128]{0,1,2:T(8,128)} fusion(bf16[16,32,128]{1,0,2:T(8,128)(2,1)} %copy.101, bf16[128,32,128]{1,0,2:T(8,128)(2,1)} %copy.102), kind=kOutput, calls=%fused_computation.4 | convolution fusion | flops 16777216 | bytes 2228224 | tf_op jit(solution)/shard_map/jkc,ikc->jic/dot_general | solution.py:117
  186.2 2.8 %copy.103 = f32[128,16,128]{2,1,0:T(8,128)} copy(f32[128,16,128]{0,1,2:T(8,128)} %convolution_bitcast_fusion) | data formatting | bytes 2097152 | tf_op jit(solution)/shard_map/jkc,ikc->jic/transpose | solution.py:117
  189.0 23.7 %reduce-scatter.2.cloned.1.call-done = f32[32,16,128]{2,1,0:T(8,128)} async-done(((f32[128,16,128]{2,1,0:T(8,128)}), f32[32,16,128]{2,1,0:T(8,128)}) %reduce-scatter.2.cloned.1.call-update) | async-done | bytes 262160 | tf_op jit(solution)/shard_map/reduce_scatter | solution.py:116
  212.7 1.1 bitcast_reduce_fusion
  213.9 1.2 multiply_reduce_fusion.1
  215.3 1.2 multiply_convert_fusion.1
  216.5 1.3 fusion.95
  218.7 1.3 fusion.4
  220.0 1.6 add_convert_fusion
  (78 shorter events, 10.0 us)
Async XLA Ops:
  7.2 12.8 %copy-start = (bf16[1024,4,256]{2,1,0:T(4,128)(2,1)S(1)}, bf16[1024,4,256]{2,1,0:T(4,128)(2,1)}, u32[]{:S(2)}) copy-start(bf16[1024,4,256]{2,1,0:T(4,128)(2,1)} %param.18) | copy-start | bytes 6291460
  9.6 75.9 %copy-start.10 = (f32[32]{0:T(128)S(1)}, f32[32]{0:T(128)}, u32[]{:S(2)}) copy-start(f32[32]{0:T(128)} %param.21) | copy-start | bytes 388
  11.8 73.8 %all-to-all-start = ((f32[4,1,4096]{2,1,0:T(1,128)}), f32[4,1,4096]{2,1,0:T(1,128)S(1)}, u32[]{:S(2)}, u32[]{:S(2)}) async-start(f32[4,1,4096]{2,1,0:T(1,128)} %reshape.259), calls=%async_computation | async-start | bytes 131072 | tf_op jit(solution)/shard_map/all_to_all | solution.py:41
  16.0 157.3 %all-gather.4.cloned.1.call-start = ((), (), s32[]{:S(2)}) async-start(), calls=%async_computation.2 | async-start | bytes 1179648 | tf_op jit(solution)/shard_map/all_gather | solution.py:115
  20.0 69.8 %copy-start.5 = (bf16[256,1024]{1,0:T(8,128)(2,1)S(1)}, bf16[256,1024]{1,0:T(8,128)(2,1)}, u32[]{:S(2)}) copy-start(bf16[256,1024]{1,0:T(8,128)(2,1)} %param.19) | copy-start | bytes 1572868
  21.9 72.2 %copy-start.6 = (bf16[128,5,128]{2,0,1:T(8,128)(2,1)S(1)}, bf16[128,5,128]{2,0,1:T(8,128)(2,1)}, u32[]{:S(2)}) copy-start(bf16[128,5,128]{2,0,1:T(8,128)(2,1)} %param.24) | copy-start | bytes 491524
  21.9 74.5 %copy-start.4 = (bf16[16,1024]{1,0:T(8,128)(2,1)S(1)}, bf16[16,1024]{1,0:T(8,128)(2,1)}, u32[]{:S(2)}) copy-start(bf16[16,1024]{1,0:T(8,128)(2,1)} %param.14) | copy-start | bytes 98308
  86.9 40.8 %copy-start.3 = (bf16[16,32,128]{2,1,0:T(8,128)(2,1)S(1)}, bf16[16,32,128]{2,1,0:T(8,128)(2,1)}, u32[]{:S(2)}) copy-start(bf16[16,32,128]{2,1,0:T(8,128)(2,1)} %param.15) | copy-start | bytes 393220
  87.4 9.3 %copy-start.8 = (bf16[1024,128]{1,0:T(8,128)(2,1)S(1)}, bf16[1024,128]{1,0:T(8,128)(2,1)}, u32[]{:S(2)}) copy-start(bf16[1024,128]{1,0:T(8,128)(2,1)} %param.22) | copy-start | bytes 786436
  90.7 1.3 collective-permute-start
  92.0 4.4 %collective-permute-start.1 = (f32[16,1024]{1,0:T(8,128)S(1)}, f32[16,1024]{1,0:T(8,128)S(1)}, u32[]{:S(2)}, u32[]{:S(2)}) collective-permute-start(f32[16,1024]{1,0:T(8,128)S(1)} %add.120), channel_id=1, source_target_pairs={{0,2},{1,3},{2,0},{3,1},{4,6},{5,7},{6,4},{7,5},{8,10},{9,11},{10,... | collective-permute-start | bytes 196616 | tf_op jit(solution)/shard_map/ppermute | solution.py:82
  96.5 32.6 %copy-start.7 = (bf16[16,1024]{1,0:T(8,128)(2,1)}, bf16[16,1024]{1,0:T(8,128)(2,1)S(1)}, u32[]{:S(2)}) copy-start(bf16[16,1024]{1,0:T(8,128)(2,1)S(1)} %get-tuple-element.3) | copy-start | bytes 98308
  128.8 0.7 copy-start.2
  131.6 81.0 %reduce-scatter.2.cloned.1.call-start = ((), (), s32[]{:S(2)}) async-start(), calls=%async_computation.3 | async-start | bytes 1310720 | tf_op jit(solution)/shard_map/reduce_scatter | solution.py:116
  216.4 2.2 copy-start.9
  217.8 0.7 copy-start.1
Sparse Core Ops, SparseCore 0:
  131.8 41.5 all-gather.3
  189.1 23.5 reduce-scatter.1
